TPU v7x, 32 devices: a whole 2x2x4 slice. The times are simulated.
32 devices in a mesh: gx: 2 (over y), gy: 4 (over x, core), gz: 4 (over z).
Axes of the slice: x: 2, y: 2, z: 4, core: 2. Of those that a mesh axis runs over, the one named last changes fastest.
Arguments:
- snapshots: bfloat16 [16, 64, 64, 256], P('gx', 'gy', 'gz'), may hold values from -1500 to 1500
- sketch: float32 [256, 256], replicated, may hold values from -0.5 to 1.5
- velocity: float32 [3, 16, 64, 64], P(None, 'gx', 'gy', 'gz'), may hold values from -4 to 4
- viscosity: float32 [16, 64, 64], P('gx', 'gy', 'gz'), may hold values from 0.2 to 2
Outputs:
- applied_modes: bfloat16 [16, 64, 64, 256], P('gx', 'gy', 'gz')
- reduced: float32 [256, 256], replicated
All inputs are finite; a program needn't handle non-finite values.
Results may differ from a plain program's by a relative error of at most 0.0015.
The roundings to bfloat16 on the way count: a program that leaves them out, or rounds other values in their place, can miss the bound.
Values may be sent and summed in bfloat16 or wider, within the bound.
No kernel may reach another device: no remote copies, remote signals or barrier semaphores. Data moves between devices by JAX's collectives and lax.ppermute only.
A program may use at most 64 MiB of HBM per device.

v0:
```python
import jax
import jax.numpy as jnp
from jax import lax
from jax.sharding import PartitionSpec as P


def padded_2(cells, sides, width):
    for axis, dim in sides:
        count = lax.axis_size(axis)
        ends = count - 1
        head = lax.slice_in_dim(cells, 0, width, axis=dim)
        tail = lax.slice_in_dim(cells, cells.shape[dim] - width, cells.shape[dim], axis=dim)
        cells = jnp.concatenate(
            [
                lax.ppermute(tail, axis, [(i, (i + 1) % count) for i in range(ends)]),
                cells,
                lax.ppermute(head, axis, [((i + 1) % count, i) for i in range(ends)]),
            ],
            axis=dim,
        )
    return cells


def apply_operator(padded, velocity, viscosity):
    centre = padded[1:-1, 1:-1, 1:-1]
    east_side = padded[2:, 1:-1, 1:-1]
    west_side = padded[:-2, 1:-1, 1:-1]
    north_side = padded[1:-1, 2:, 1:-1]
    south_side = padded[1:-1, :-2, 1:-1]
    upper_side = padded[1:-1, 1:-1, 2:]
    lower_side = padded[1:-1, 1:-1, :-2]
    neighbours = east_side + west_side + north_side + south_side + upper_side + lower_side
    viscous_term = viscosity[..., None] * (6.0 * centre - neighbours)
    flow_term = velocity[0][..., None] * (east_side - west_side)
    flow_term = flow_term + velocity[1][..., None] * (north_side - south_side)
    flow_term = flow_term + velocity[2][..., None] * (upper_side - lower_side)
    return viscous_term + 0.5 * flow_term


def inner_rows(left_rows, right_rows, precision):
    return lax.dot_general(
        left_rows,
        right_rows,
        (((0,), (0,)), ((), ())),
        precision=precision,
        preferred_element_type=jnp.float32,
    )


def per_device(snapshots, sketch, velocity, viscosity):
    highest = lax.Precision.HIGHEST
    columns = sketch.shape[0]
    cells_x, cells_y, cells_z = (snapshots.shape[0], snapshots.shape[1], snapshots.shape[2])
    ncells = (
        cells_x
        * cells_y
        * cells_z
        * lax.axis_size("gx")
        * lax.axis_size("gy")
        * lax.axis_size("gz")
    )
    sketched = jnp.dot(
        snapshots.reshape(-1, columns).astype(jnp.float32), sketch, precision=highest
    ).astype(jnp.bfloat16)
    local_gram = inner_rows(sketched, sketched, None) / ncells
    gram_matrix = lax.psum(local_gram, ("gx", "gy", "gz"))
    lower_factor = jnp.linalg.cholesky(gram_matrix)
    inverse = jax.scipy.linalg.solve_triangular(
        lower_factor, jnp.eye(columns, dtype=jnp.float32), lower=True
    )
    mode_rows = jnp.dot(sketched.astype(jnp.float32), inverse.T, precision=highest)
    mode_field = mode_rows.reshape(cells_x, cells_y, cells_z, columns)
    padded_modes = padded_2(mode_field, (("gx", 0), ("gy", 1), ("gz", 2)), 1)
    image_rows = apply_operator(padded_modes, velocity, viscosity).reshape(-1, columns)
    local_reduced = inner_rows(mode_rows, image_rows, highest) / ncells
    reduced = lax.psum(local_reduced, ("gx", "gy", "gz"))
    applied_modes = image_rows.reshape(cells_x, cells_y, cells_z, columns).astype(jnp.bfloat16)
    return (applied_modes, reduced)


def solution(mesh):
    in_specs = (P("gx", "gy", "gz", None), P(), P(None, "gx", "gy", "gz"), P("gx", "gy", "gz"))
    out_specs = (P("gx", "gy", "gz", None), P())
    return jax.shard_map(
        per_device, mesh=mesh, in_specs=in_specs, out_specs=out_specs, check_vma=False
    )
```

profile of v0, /device:TPU:0, one launch (start us, length us, event | category | flops | bytes accessed | tf_op | source)
XLA Modules:
  0.0 380.9 jit_solution(7893172982498539869)
XLA Ops:
  7.2 1.2 copy-done
  8.4 2.0 convolution_convert_fusion
  10.4 1.2 convolution_multiply_fusion.1
  11.7 131.6 %all-reduce.4.cloned.1.call-done = f32[256,256]{0,1:T(8,128)} async-done(((f32[256,256]{0,1:T(8,128)}), f32[256,256]{0,1:T(8,128)}) %all-reduce.4.cloned.1.call-update) | async-done | bytes 262160 | tf_op jit(solution)/shard_map/psum | solution.py:66
  143.3 1.1 copy.7
  144.4 1.0 fusion.4
  145.4 11.7 %cholesky.50 = f32[128,128]{1,0:T(8,128)S(1)} custom-call(f32[128,128]{1,0:T(8,128)S(1)} %cholesky.118), custom_call_target="Cholesky" | custom-call | tf_op jit(solution)/shard_map/jit(cholesky)/cholesky | solution.py:67
  157.2 9.8 %custom-call.15 = f32[1,128,128]{1,2,0:T(8,128)S(1)} custom-call(f32[1,128,128]{2,1,0:T(8,128)S(1)} %get-tuple-element.36), custom_call_target="InvertDiagBlocksLowerTriangular" | custom-call | tf_op jit(solution)/shard_map/jit(cholesky)/cholesky | solution.py:67
  167.5 11.7 %cholesky.105 = f32[128,128]{1,0:T(8,128)S(1)} custom-call(f32[128,128]{1,0:T(8,128)S(1)} %convolution_subtract_fusion.1), custom_call_target="Cholesky" | custom-call | tf_op jit(solution)/shard_map/jit(cholesky)/cholesky | solution.py:67
  179.2 0.7 compare_reduce_fusion
  181.4 4.2 %while.1 = (s32[]{:T(128)}, f32[256,256]{1,0:T(8,128)S(1)}, s32[2,2]{1,0:T(2,128)S(1)}, f32[2,128,128]{2,1,0:T(8,128)S(1)}, s32[]{:T(128)}) while((s32[]{:T(128)}, f32[256,256]{1,0:T(8,128)S(1)}, s32[2,2]{1,0:T(2,128)S(1)}, f32[2,128,128]{2,1,0:T(8,128)S(1)}, s32[]{:T(128)}) %tuple.34), condition=%wide.while_cond, body=%wide.while_body.sunk | while | flops 2 | bytes 131189 | solution.py:68
  181.5 0.6 fusion.28
  182.1 1.4 bitcast_dynamic-update-slice_fusion.2
  183.6 0.6 fusion.28
  184.2 1.4 bitcast_dynamic-update-slice_fusion.2
  185.6 19.7 %custom-call.16 = f32[2,128,128]{1,2,0:T(8,128)S(1)} custom-call(f32[2,128,128]{2,1,0:T(8,128)S(1)} %get-tuple-element.9), custom_call_target="InvertDiagBlocksLowerTriangular" | custom-call | tf_op jit(solution)/shard_map/jit(_solve_triangular)/triangular_solve | solution.py:68
  206.1 1.1 fusion
  207.2 1.3 collective-permute-start
  208.5 4.6 %collective-permute-start.1 = (f32[1,16,16,256]{3,2,1,0:T(8,128)S(1)}, f32[1,16,16,256]{3,2,1,0:T(8,128)S(1)}, u32[]{:S(2)}, u32[]{:S(2)}) collective-permute-start(f32[1,16,16,256]{3,2,1,0:T(8,128)S(1)} %bitcast.54), channel_id=1, source_target_pairs={{0,16},{1,17},{2,18},{3,19},{4,20},{5,21},{6,22},{7,23},{8,24},{9,... | collective-permute-start | bytes 786440 | tf_op jit(solution)/shard_map/ppermute | solution.py:15
  213.1 3.3 collective-permute-done
  216.4 1.2 collective-permute-done.1
  217.6 1.4 collective-permute-start.3
  219.1 1.3 collective-permute-start.2
  220.4 3.7 collective-permute-done.2
  224.3 1.3 collective-permute-start.4
  225.6 4.6 %collective-permute-start.5 = (f32[10,18,1,256]{3,2,1,0:T(1,128)S(1)}, f32[10,18,1,256]{3,2,1,0:T(1,128)S(1)}, u32[]{:S(2)}, u32[]{:S(2)}) collective-permute-start(f32[10,18,1,256]{3,2,1,0:T(1,128)S(1)} %get-tuple-element.25), channel_id=1, source_target_pairs={{0,1},{1,2},{2,3},{4,5},{5,6},{6,7},{8,9},{9,10},{10,11},{12,13},{... | collective-permute-start | bytes 552968 | tf_op jit(solution)/shard_map/ppermute | solution.py:15
  230.2 1.5 collective-permute-done.4
  231.7 1.5 collective-permute-done.5
  233.2 4.6 %fusion.13 = (bf16[8,16,16,256]{3,2,1,0:T(8,128)(2,1)}, f32[8,16,16,256]{3,2,1,0:T(8,128)S(1)}) fusion(f32[8,16,16]{2,1,0:T(8,128)S(1)} %get-tuple-element.31, f32[8,16,16]{2,1,0:T(8,128)S(1)} %get-tuple-element.32, f32[8,16,16]{2,1,0:T(8,128)S(1)} %get-tuple-element.30, f32[10,1,16,256]{3,2,1,0:T(8,128)S(1)} %collective-permute-done.2, ...), kind=kLoop, calls=%fused_computation.66 | loop fusion | flops 19398656 | bytes 6496256 | tf_op jit(solution)/shard_map/convert_element_type | solution.py:77
  237.8 4.3 %convolution_multiply_fusion = f32[256,256]{0,1:T(8,128)} fusion(f32[2048,256]{1,0:T(8,128)S(1)} %fusion, f32[2048,256]{1,0:T(8,128)S(1)} %bitcast.53), kind=kOutput, calls=%fused_computation.22 | convolution fusion | flops 1610678272 | bytes 4456448 | tf_op jit(solution)/shard_map/dot_general | solution.py:41
  242.1 130.2 %all-reduce.6.cloned.1.call-done = f32[256,256]{0,1:T(8,128)} async-done(((f32[256,256]{0,1:T(8,128)}), f32[256,256]{0,1:T(8,128)}) %all-reduce.6.cloned.1.call-update) | async-done | bytes 262160 | tf_op jit(solution)/shard_map/psum | solution.py:76
  372.3 1.8 copy.9
  (30 shorter events, 2.0 us)
Async XLA Ops:
  7.2 1.2 copy-start
  7.2 136.1 %all-reduce.4.cloned.1.call-start = ((), (), s32[]{:S(2)}) async-start(), calls=%async_computation | async-start | bytes 524288 | tf_op jit(solution)/shard_map/psum | solution.py:66
  11.6 360.7 %all-reduce.6.cloned.1.call-start = ((), (), s32[]{:S(2)}) async-start(), calls=%async_computation.1 | async-start | bytes 524288 | tf_op jit(solution)/shard_map/psum | solution.py:76
  207.2 9.1 %collective-permute-start = (f32[1,16,16,256]{3,2,1,0:T(8,128)S(1)}, f32[1,16,16,256]{3,2,1,0:T(8,128)S(1)}, u32[]{:S(2)}, u32[]{:S(2)}) collective-permute-start(f32[1,16,16,256]{3,2,1,0:T(8,128)S(1)} %bitcast.55), channel_id=1, source_target_pairs={{16,0},{17,1},{18,2},{19,3},{20,4},{21,5},{22,6},{23,7},{24,8},{25... | collective-permute-start | bytes 786440 | tf_op jit(solution)/shard_map/ppermute | solution.py:17
  208.5 9.0 %collective-permute-start.1 = (f32[1,16,16,256]{3,2,1,0:T(8,128)S(1)}, f32[1,16,16,256]{3,2,1,0:T(8,128)S(1)}, u32[]{:S(2)}, u32[]{:S(2)}) collective-permute-start(f32[1,16,16,256]{3,2,1,0:T(8,128)S(1)} %bitcast.54), channel_id=1, source_target_pairs={{0,16},{1,17},{2,18},{3,19},{4,20},{5,21},{6,22},{7,23},{8,24},{9,... | collective-permute-start | bytes 786440 | tf_op jit(solution)/shard_map/ppermute | solution.py:15
  217.6 12.6 %copy-start.1 = (f32[3,8,16,16]{3,2,1,0:T(8,128)S(1)}, f32[3,8,16,16]{3,2,1,0:T(8,128)}, u32[]{:S(2)}) copy-start(f32[3,8,16,16]{3,2,1,0:T(8,128)} %param.6) | copy-start | bytes 73732
  217.6 15.6 %copy-start.2 = (f32[8,16,16]{2,1,0:T(8,128)S(1)}, f32[8,16,16]{2,1,0:T(8,128)}, u32[]{:S(2)}) copy-start(f32[8,16,16]{2,1,0:T(8,128)} %param.7) | copy-start | bytes 24580
  217.6 2.7 collective-permute-start.3
  219.1 5.0 %collective-permute-start.2 = (f32[10,1,16,256]{3,2,1,0:T(8,128)S(1)}, f32[10,1,16,256]{3,2,1,0:T(8,128)S(1)}, u32[]{:S(2)}, u32[]{:S(2)}) collective-permute-start(f32[10,1,16,256]{3,2,1,0:T(8,128)S(1)} %get-tuple-element.27), channel_id=1, source_target_pairs={{4,0},{8,4},{12,8},{5,1},{9,5},{13,9},{6,2},{10,6},{14,10},{7,3},{... | collective-permute-start | bytes 491528 | tf_op jit(solution)/shard_map/ppermute | solution.py:17
  224.3 7.4 %collective-permute-start.4 = (f32[10,18,1,256]{3,2,1,0:T(1,128)S(1)}, f32[10,18,1,256]{3,2,1,0:T(1,128)S(1)}, u32[]{:S(2)}, u32[]{:S(2)}) collective-permute-start(f32[10,18,1,256]{3,2,1,0:T(1,128)S(1)} %get-tuple-element.24), channel_id=1, source_target_pairs={{1,0},{2,1},{3,2},{5,4},{6,5},{7,6},{9,8},{10,9},{11,10},{13,12},{... | collective-permute-start | bytes 552968 | tf_op jit(solution)/shard_map/ppermute | solution.py:17
  225.6 7.6 %collective-permute-start.5 = (f32[10,18,1,256]{3,2,1,0:T(1,128)S(1)}, f32[10,18,1,256]{3,2,1,0:T(1,128)S(1)}, u32[]{:S(2)}, u32[]{:S(2)}) collective-permute-start(f32[10,18,1,256]{3,2,1,0:T(1,128)S(1)} %get-tuple-element.25), channel_id=1, source_target_pairs={{0,1},{1,2},{2,3},{4,5},{5,6},{6,7},{8,9},{9,10},{10,11},{12,13},{... | collective-permute-start | bytes 552968 | tf_op jit(solution)/shard_map/ppermute | solution.py:15
Sparse Core Ops, SparseCore 0:
  14.1 129.2 all-reduce.3
  242.2 130.0 all-reduce.5
where the time goes:
time: 381 us
  waiting for transfers between devices  273 us (72%)
  other arithmetic  59.6 us (16%)
  between operations  15.6 us (4%)
  starting transfers between devices  14.5 us (4%)
  matrix products  9.81 us (3%)
  local copies, waits for them, and re-layouts  8.22 us (2%)
    psum x1, waiting for transfers between devices, per_device(): gram_matrix = lax.psum(local_gram, ('gx', 'gy', 'gz'))  132 us
    psum x1, waiting for transfers between devices, per_device(): reduced = lax.psum(local_reduced, ('gx', 'gy', 'gz'))  130 us
    another operation x6, other arithmetic, per_device(): lower_factor = jnp.linalg.cholesky(gram_matrix)  34 us
    another operation x3, other arithmetic, per_device(): jax.scipy.linalg.solve_triangular(lower_factor, jnp.eye(columns, dtype=jn...  19.7 us
    ppermute x3, starting transfers between devices, padded_2(): lax.ppermute(tail, axis, [(i, (i + 1) % count) for i in range(ends)])  10.6 us
    ppermute x3, waiting for transfers between devices, padded_2(): lax.ppermute(head, axis, [((i + 1) % count, i) for i in range(ends)])  8.48 us
  transfers between devices with their start and end apart: 8, of which 7 were waited for; matrix products, arithmetic and copies ran while one was open for 0% of the time, Pallas kernels for 0%

commit v1 on v0

v1 whole, which is shorter than its diff:
```python
import functools

import jax
import jax.numpy as jnp
from jax import lax
from jax.experimental import pallas as pl
from jax.experimental.pallas import tpu as pltpu
from jax.sharding import PartitionSpec as P

f32 = jnp.float32
bf16 = jnp.bfloat16
VMEM = pl.BlockSpec(memory_space=pltpu.VMEM)
SMEM = pl.BlockSpec(memory_space=pltpu.SMEM)
HBM = pl.BlockSpec(memory_space=pltpu.HBM)
PARAMS = pltpu.CompilerParams(vmem_limit_bytes=16 << 20)
TILE = 8
PANEL = 64


def split2(x):
    high = x.astype(bf16)
    return high, (x - high.astype(f32)).astype(bf16)


def split3(x):
    high = x.astype(bf16)
    return (high, *split2(x - high.astype(f32)))


def matmul(a, b, dim_a, dim_b):
    return lax.dot_general(a, b, (((dim_a,), (dim_b,)), ((), ())), preferred_element_type=f32)


def dot_f32(a, b, dim_a, dim_b):
    ah, am, al = split3(a)
    bh, bm, bl = split3(b)
    left = jnp.concatenate([ah, ah, am, am, ah, al], axis=dim_a)
    right = jnp.concatenate([bh, bm, bh, bm, bl, bh], axis=dim_b)
    return matmul(left, right, dim_a, dim_b)


def on_chip(shape, dtype):
    return pltpu.VMEM(shape, dtype)


def in_hbm(*values):
    return [pltpu.with_memory_space_constraint(value, pltpu.HBM) for value in values]


def held(*values):
    return [pltpu.with_memory_space_constraint(value, pltpu.VMEM) for value in values]


def sketch_kernel(
    scale,
    steps,
    flag_ref,
    snap_ref,
    sketch_ref,
    out_ref,
    x1_ref,
    x2_ref,
    y1_ref,
    y2_ref,
    z1_ref,
    z2_ref,
    sent_ref,
    kept_ref,
    rows_ref,
    table_ref,
    parts_ref,
    gram_ref,
    sems,
):
    cells_x, cells_y, cells_z, columns = out_ref.shape
    half = columns // 2
    planes = cells_x // steps
    table = pltpu.make_async_copy(sketch_ref, table_ref, sems.at[steps])
    table.start()
    copies = []
    for i in range(steps):
        span = pl.ds(i * planes, planes)
        copies.append(pltpu.make_async_copy(snap_ref.at[span], rows_ref.at[span], sems.at[i]))
        copies[-1].start()
    table.wait()
    for i, part in enumerate(split3(table_ref[...])):
        parts_ref[i * columns : (i + 1) * columns, :] = part
    even = [flag_ref[k] == 0 for k in range(3)]
    for i in range(steps):
        copies[i].wait()
        span = slice(i * planes, (i + 1) * planes)
        rows = rows_ref[span].reshape(-1, columns)
        made = matmul(jnp.concatenate([rows, rows, rows], axis=1), parts_ref[...], 1, 0)
        made = made.astype(bf16)
        gram = matmul(made, made, 0, 0)
        for at, value in (
            (0, gram[:half, :half]),
            (half, gram[:half, half:]),
            (columns, gram[half:, half:]),
        ):
            value = value if i == 0 else gram_ref[at : at + half, :] + value
            gram_ref[at : at + half, :] = value * scale if i == steps - 1 else value
        out_ref[span] = made.reshape(planes, cells_y, cells_z, columns)
        field = out_ref[span]
        low_y, high_y = field[:, 0], field[:, cells_y - 1]
        y1_ref[span] = jnp.where(even[1], high_y, low_y)
        y2_ref[span] = jnp.where(even[1], low_y, high_y)
        low_z = field[:, :, 0, :].astype(f32)
        high_z = field[:, :, cells_z - 1, :].astype(f32)
        z1_ref[span] = jnp.where(even[2], high_z, low_z).astype(bf16)
        z2_ref[span] = jnp.where(even[2], low_z, high_z).astype(bf16)
    low_x, high_x = out_ref[0], out_ref[cells_x - 1]
    x1_ref[...] = jnp.where(even[0], high_x, low_x)
    x2_ref[...] = jnp.where(even[0], low_x, high_x)
    size = sent_ref.shape[0]
    mine = pl.multiple_of(flag_ref[3] * size, size)
    other = pl.multiple_of((1 - flag_ref[3]) * size, size)
    kept_ref[...] = gram_ref[pl.ds(mine, size), :]
    sent_ref[...] = gram_ref[pl.ds(other, size), :]


def sketch_call(flags, snapshots, sketch, scale):
    cells_x, cells_y, cells_z, columns = snapshots.shape
    half = columns // 2
    steps = 4
    return pl.pallas_call(
        functools.partial(sketch_kernel, scale, steps),
        in_specs=[SMEM, HBM, HBM],
        out_specs=[VMEM] * 9,
        out_shape=[
            on_chip(snapshots.shape, bf16),
            on_chip((cells_y, cells_z, columns), bf16),
            on_chip((cells_y, cells_z, columns), bf16),
            on_chip((cells_x, cells_z, columns), bf16),
            on_chip((cells_x, cells_z, columns), bf16),
            on_chip((cells_x, cells_y, columns), bf16),
            on_chip((cells_x, cells_y, columns), bf16),
            on_chip((3 * half // 2, half), f32),
            on_chip((3 * half // 2, half), f32),
        ],
        scratch_shapes=[
            pltpu.VMEM(snapshots.shape, bf16),
            pltpu.VMEM(sketch.shape, f32),
            pltpu.VMEM((3 * columns, columns), bf16),
            pltpu.VMEM((3 * half, half), f32),
            pltpu.SemaphoreType.DMA((steps + 1,)),
        ],
        compiler_params=PARAMS,
        name="sketch",
    )(flags, *in_hbm(snapshots, sketch))


def operator_kernel(
    scale,
    planes,
    flag_ref,
    s_ref,
    x1_ref,
    x2_ref,
    y1_ref,
    y2_ref,
    z1_ref,
    z2_ref,
    coef_ref,
    *refs,
):
    cells_x, cells_y, _, columns = s_ref.shape
    first = planes[0]
    even = [flag_ref[k] == 0 for k in range(3)]
    if first == 0:
        image_ref, total_ref = refs
    else:
        sum_ref, image_ref, sent_ref, kept_ref, total_ref = refs
    for x in planes:
        plane = s_ref[x]
        if x > 0:
            before = s_ref[x - 1]
        else:
            before = jnp.where(even[0], x2_ref[...], x1_ref[...])
        if x < cells_x - 1:
            after = s_ref[x + 1]
        else:
            after = jnp.where(even[0], x1_ref[...], x2_ref[...])
        before, after, middle = before.astype(f32), after.astype(f32), plane.astype(f32)
        y1, y2 = y1_ref[x].astype(f32), y2_ref[x].astype(f32)
        z1, z2 = z1_ref[x].astype(f32), z2_ref[x].astype(f32)
        south = jnp.concatenate([jnp.where(even[1], y2, y1)[None], middle[:-1]], axis=0)
        north = jnp.concatenate([middle[1:], jnp.where(even[1], y1, y2)[None]], axis=0)
        below = jnp.where(even[2], z2, z1)[:, None, :]
        above = jnp.where(even[2], z1, z2)[:, None, :]
        lower = jnp.concatenate([below, middle[:, :-1]], axis=1)
        upper = jnp.concatenate([middle[:, 1:], above], axis=1)
        around = (after + before) + (north + south) + (upper + lower)

        def spread(k):
            return jnp.stack([coef_ref[k, x, :, y : y + 1] for y in range(cells_y)], axis=0)

        image = spread(3) * (6.0 * middle - around)
        image = image + spread(0) * (after - before)
        image = image + spread(1) * (north - south)
        image = image + spread(2) * (upper - lower)
        high, low = split2(image.reshape(-1, columns))
        count = high.shape[0]
        at = (x - first) * count
        image_ref[at : at + count, :columns] = high
        image_ref[at : at + count, columns:] = low
        base = plane.reshape(-1, columns)
        part = matmul(
            jnp.concatenate([base, base], axis=0), jnp.concatenate([high, low], axis=0), 0, 0
        )
        if x > first:
            part = total_ref[...] + part
        elif first > 0:
            part = sum_ref[...] + part
        if x < cells_x - 1:
            total_ref[...] = part
        else:
            total_ref[...] = part * scale
            size = columns // 2
            mine = pl.multiple_of(flag_ref[3] * size, size)
            other = pl.multiple_of((1 - flag_ref[3]) * size, size)
            for at in (0, size):
                kept_ref[at : at + size, :] = total_ref[pl.ds(mine, size), at : at + size]
                sent_ref[at : at + size, :] = total_ref[pl.ds(other, size), at : at + size]


def operator_calls(flags, sketched, halos, coefs, scale):
    cells_x, cells_y, cells_z, columns = sketched.shape
    half = cells_x // 2
    image = on_chip((half * cells_y * cells_z, 2 * columns), bf16)
    image0, partial = pl.pallas_call(
        functools.partial(operator_kernel, scale, range(half)),
        in_specs=[SMEM] + [VMEM] * 8,
        out_specs=[VMEM] * 2,
        out_shape=[image, on_chip((columns, columns), f32)],
        compiler_params=PARAMS,
        name="operator0",
    )(flags, *held(sketched, *halos, coefs))
    image1, sent, kept = pl.pallas_call(
        functools.partial(operator_kernel, scale, range(half, cells_x)),
        in_specs=[SMEM] + [VMEM] * 9,
        out_specs=[VMEM] * 3,
        out_shape=[image] + [on_chip((columns, columns // 2), f32)] * 2,
        scratch_shapes=[pltpu.VMEM((columns, columns), f32)],
        compiler_params=PARAMS,
        name="operator1",
    )(flags, *held(sketched, *halos, coefs, partial))
    return image0, image1, sent, kept


def eliminate(block):
    size = block.shape[0]
    sub = lax.broadcasted_iota(jnp.int32, (TILE, size), 0)
    lane = lax.broadcasted_iota(jnp.int32, (TILE, size), 1)
    tiles = [block[i : i + TILE, :] for i in range(0, size, TILE)]
    count = size // TILE
    pivots = []

    def full(value):
        return jnp.broadcast_to(value, (TILE, size))

    for s in range(count):
        at = s * TILE
        tile = tiles[s]
        cols = [
            [full(tiles[t][:, at + k : at + k + 1]) for k in range(TILE)] for t in range(s, count)
        ]
        a = [[full(cols[0][k][i : i + 1, :]) for k in range(i + 1)] for i in range(TILE)]
        w = [[None] * TILE for _ in range(TILE)]
        r = []
        for j in range(TILE):
            r.append(1.0 / a[j][j])
            m = [a[i][j] * r[j] if i > j else None for i in range(TILE)]
            for i in range(j + 1, TILE):
                for k in range(j + 1, i + 1):
                    a[i][k] = a[i][k] - m[i] * a[k][j]
                for k in range(j):
                    w[i][k] = w[i][k] - m[i] * w[j][k]
                w[i][j] = -m[i]
        unit = []
        for k in range(TILE):
            col = jnp.where(sub == k, 1.0, 0.0)
            for i in range(k + 1, TILE):
                col = jnp.where(sub == i, w[i][k], col)
            unit.append(col)
        pivot = r[0]
        for i in range(1, TILE):
            pivot = jnp.where(sub == i, r[i], pivot)
        pivots.append(pivot[:, :1])
        new = unit[0] * full(tile[:1, :])
        for k in range(1, TILE):
            new = new + unit[k] * full(tile[k : k + 1, :])
        for k in range(TILE):
            new = jnp.where(lane == at + k, unit[k], new)
        tiles[s] = new
        if s == count - 1:
            break
        rows = [full(new[k : k + 1, :]) for k in range(TILE)]
        inside = (lane >= at) & (lane < at + TILE)
        for t in range(s + 1, count):
            col = cols[t - s]
            left = jnp.where(inside, 0.0, tiles[t])
            for k in range(TILE):
                factor = col[k]
                for i in range(k):
                    factor = factor + w[k][i] * col[i]
                left = left - (factor * r[k]) * rows[k]
            tiles[t] = left
    result = jnp.concatenate(tiles, axis=0)
    row_b = lax.broadcasted_iota(jnp.int32, (size, size), 0)
    lane_b = lax.broadcasted_iota(jnp.int32, (size, size), 1)
    return jnp.where(lane_b <= row_b, result, 0.0), jnp.concatenate(pivots, axis=0)


def factor_kernel(start, *refs):
    if start == 0:
        flag_ref, part_ref, other_ref, out_ref, next_ref, state_ref = refs
        half = state_ref.shape[1] // 2
        own_first = flag_ref[3] == 0
        part, other = part_ref[...], other_ref[...]
        upper = jnp.where(own_first, part, other)
        under = jnp.where(own_first, other, part)
        both = jnp.concatenate([upper, under], axis=0)
        state_ref[:half, :half] = both[:half]
        state_ref[:half, half:] = both[half : 2 * half]
        state_ref[half:, :half] = jnp.zeros((half, half), f32)
        state_ref[half:, half:] = both[2 * half :]
    elif len(refs) == 3:
        state_ref, out_ref, next_ref = refs
    else:
        state_ref, out_ref = refs
        next_ref = None
    n = state_ref.shape[1]
    end = start + PANEL
    lane = lax.broadcasted_iota(jnp.int32, (PANEL, n), 1)
    unit, pivots = eliminate(state_ref[:PANEL, start:end])
    panel = dot_f32(unit, state_ref[:PANEL, :], 1, 0)
    pieces = [unit]
    if start:
        pieces = [jnp.zeros((PANEL, start), f32)] + pieces
    if end < n:
        pieces = pieces + [jnp.zeros((PANEL, n - end), f32)]
    inside = (lane >= start) & (lane < end)
    rows = jnp.where(inside, jnp.concatenate(pieces, axis=1), panel)
    out_ref[...] = jnp.where(lane < end, rows * jnp.sqrt(pivots), 0.0)
    if end < n:
        factors = (panel * pivots)[:, end:]
        lane_r = lax.broadcasted_iota(jnp.int32, (n - end, n), 1)
        old = jnp.where((lane_r >= start) & (lane_r < end), 0.0, state_ref[PANEL:, :])
        next_ref[...] = old - dot_f32(factors, rows, 0, 0)


def factor_calls(flags, part, other):
    n = part.shape[1] * 2
    rows = []
    state = None
    for start in range(0, n, PANEL):
        left = n - start - PANEL
        outs = [on_chip((PANEL, n), f32)]
        if left:
            outs.append(on_chip((left, n), f32))
        args = (flags, *held(part, other)) if start == 0 else held(state)
        got = pl.pallas_call(
            functools.partial(factor_kernel, start),
            in_specs=[SMEM, VMEM, VMEM] if start == 0 else [VMEM],
            out_specs=[VMEM] * len(outs),
            out_shape=outs,
            scratch_shapes=[pltpu.VMEM((n, n), f32)] if start == 0 else [],
            compiler_params=PARAMS,
        )(*args)
        rows.append(got[0])
        if left:
            state = got[1]
    return rows


def finish_kernel(steps, flag_ref, part_ref, other_ref, image0_ref, image1_ref, *refs):
    count = len(refs) - 5
    inverse_refs, (out_ref, reduced_ref, right_ref, made_ref, sems) = refs[:count], refs[count:]
    columns = out_ref.shape[1]
    half = columns // 2
    inverse = jnp.concatenate([ref[...] for ref in inverse_refs], axis=0)
    own_first = flag_ref[3] == 0
    part = jnp.concatenate([part_ref[:half, :], part_ref[half:, :]], axis=1)
    other = jnp.concatenate([other_ref[:half, :], other_ref[half:, :]], axis=1)
    gram = jnp.concatenate(
        [jnp.where(own_first, part, other), jnp.where(own_first, other, part)], axis=0
    )
    high, low = split2(inverse)
    right_ref[...] = jnp.concatenate([high, low, high], axis=1)
    right = right_ref[...]
    block = out_ref.shape[0] // steps
    copies = []

    def applied(i):
        ref, at = (image0_ref, i) if i < steps // 2 else (image1_ref, i - steps // 2)
        image = ref[at * block : (at + 1) * block, :]
        left = jnp.concatenate([image[:, :columns], image], axis=1)
        span = pl.ds(i * block, block)
        made_ref[span, :] = matmul(left, right, 1, 1).astype(bf16)
        copies.append(pltpu.make_async_copy(made_ref.at[span], out_ref.at[span], sems.at[i]))
        copies[-1].start()

    middle = dot_f32(inverse, gram, 1, 0)
    for i in range(steps - 1):
        applied(i)
    reduced_ref[...] = dot_f32(middle, inverse, 1, 1)
    applied(steps - 1)
    for copy in copies:
        copy.wait()


def finish_call(flags, part, other, image0, image1, rows):
    count, columns = image0.shape[0] * 2, image0.shape[1] // 2
    steps = 4
    return pl.pallas_call(
        functools.partial(finish_kernel, steps),
        in_specs=[SMEM] + [VMEM] * (4 + len(rows)),
        out_specs=[HBM, VMEM],
        out_shape=[
            jax.ShapeDtypeStruct((count, columns), bf16),
            jax.ShapeDtypeStruct((columns, columns), f32),
        ],
        scratch_shapes=[
            pltpu.VMEM((columns, 3 * columns), bf16),
            pltpu.VMEM((count, columns), bf16),
            pltpu.SemaphoreType.DMA((steps,)),
        ],
        compiler_params=PARAMS,
        name="finish",
    )(flags, *held(part, other, image0, image1, *rows))


AXES = ("gx", "gy", "gz")
PLANE = ("gx", "gy")


def swap(value, masks):
    depth = lax.axis_size("gz")
    pairs = [(i, i ^ masks[i // depth % 2]) for i in range(lax.axis_size(AXES))]
    return lax.ppermute(value, AXES, pairs)


def stages():
    depth = lax.axis_size("gz")
    plane, line = [], []
    mask = 2
    while mask < lax.axis_size(PLANE):
        plane.append(mask * depth)
        mask *= 2
    mask = 1
    while mask < depth:
        line.append(mask)
        mask *= 2
    bits = line[-1:] + plane + line[:-1]
    turned = list(bits)
    for k in range(0, len(bits) - 1, 2):
        turned[k], turned[k + 1] = bits[k + 1], bits[k]
    return list(zip(bits, turned))


def exchange(part, masks):
    got = swap(part, masks)
    return part + got


def trade(sent):
    depth = lax.axis_size("gz")
    return swap(sent, (depth, depth))


def halo_pair(first, second, axis):
    count = lax.axis_size(axis)
    got = []
    for start, layer in ((0, first), (1, second)):
        pairs = []
        for i in range(start, count - 1, 2):
            pairs += [(i, i + 1), (i + 1, i)]
        if pairs:
            got.append(lax.ppermute(layer, axis, pairs))
        else:
            got.append(jnp.zeros_like(layer))
    return got


def body(snapshots, sketch, velocity, viscosity):
    shape = snapshots.shape
    ncells = shape[0] * shape[1] * shape[2]
    for axis in ("gx", "gy", "gz"):
        ncells *= lax.axis_size(axis)
    scale = 1.0 / ncells
    flags = [lax.axis_index(axis) % 2 for axis in ("gx", "gy", "gz")]
    flags = jnp.stack(flags + [lax.axis_index(PLANE) % 2]).astype(jnp.int32)
    coefs = jnp.concatenate([0.5 * velocity, viscosity[None]], axis=0).transpose(0, 1, 3, 2)
    sketched, x1, x2, y1, y2, z1, z2, sent, kept = sketch_call(
        flags, snapshots, sketch, scale
    )
    steps = stages()
    ahead = min(2, len(steps))
    part = kept + trade(sent)
    for k in range(ahead):
        part = exchange(part, steps[k])
    halos = halo_pair(x1, x2, "gx") + halo_pair(y1, y2, "gy")
    halos = halos + halo_pair(z1, z2, "gz")
    image0, image1, sent, kept = operator_calls(flags, sketched, halos, coefs, scale)
    i_part = kept + trade(sent)
    size = part.shape[0]
    both = jnp.concatenate([part, i_part], axis=0)
    for k in range(ahead, len(steps)):
        both = exchange(both, steps[k])
    part, i_part = both[:size], both[size:]
    other = trade(part)
    rows = factor_calls(flags, part, other)
    for k in range(ahead):
        i_part = exchange(i_part, steps[k])
    i_other = trade(i_part)
    applied, reduced = finish_call(flags, i_part, i_other, image0, image1, rows)
    return applied.reshape(shape), reduced


def solution(mesh):
    in_specs = (P("gx", "gy", "gz", None), P(), P(None, "gx", "gy", "gz"), P("gx", "gy", "gz"))
    out_specs = (P("gx", "gy", "gz", None), P())
    return jax.shard_map(body, mesh=mesh, in_specs=in_specs, out_specs=out_specs, check_vma=False)
```

time: 381 us -> 73.2 us (0.19)
  waiting for transfers between devices: 273 us -> 24.7 us
  other arithmetic: 59.6 us -> 0.27 us
  Pallas kernels: 0 us -> 24.6 us
  between operations: 15.6 us -> 0.9 us
  matrix products: 9.81 us -> 0 us
  local copies, waits for them, and re-layouts: 8.22 us -> 1.03 us
  starting transfers between devices: 14.5 us -> 21.6 us
    psum x2 -> x0, waiting for transfers between devices: 262 us -> none  [the longest x1 132 us: per_device(): gram_matrix = lax.psum(local_gram, ('gx', 'gy', 'gz'))]
    another operation x9 -> x1, other arithmetic: 53.7 us -> 0.08 us  [body(): flags = jnp.stack(flags + [lax.axis_index(PLANE) % 2]).astype(jnp.int32)]
    pallas_call x0 -> x8, Pallas kernels: none -> 24.6 us  [the longest x4 11.2 us: factor_calls(): pl.pallas_call(functools.partial(factor_kernel, start), in_specs=[SMEM, V...]
    ppermute x6 -> x15, waiting for transfers between devices: 11.1 us -> 24.7 us  [the longest x10 24.7 us: swap(): return lax.ppermute(value, AXES, pairs)]
    dot_general x4 -> x0, matrix products: 8.51 us -> none  [the longest x2 5.5 us: inner_rows(): lax.dot_general(left_rows, right_rows, (((0,), (0,)), ((), ())), precisio...]
    ppermute x6 -> x15, starting transfers between devices: 14.4 us -> 21.6 us  [the longest x10 15.5 us: swap(): return lax.ppermute(value, AXES, pairs)]
    convert_element_type x1 -> x0, other arithmetic: 4.61 us -> none  [per_device(): image_rows.reshape(cells_x, cells_y, cells_z, columns).astype(jnp.bfloat16)]
    another operation x9 -> x0, local copies, waits for them, and re-layouts: 4.12 us -> none
  transfers between devices with their start and end apart: 8 -> 15, of which waited for: 7 -> 7; matrix products, arithmetic and copies ran while one was open for 0% -> 0% of each run, Pallas kernels for 0% -> 23%
where the time goes in v1:
time: 73.2 us; the launch traced here: 73 us
  waiting for transfers between devices  24.7 us (34%)
  Pallas kernels  24.6 us (34%)
  starting transfers between devices  21.6 us (30%)
  local copies, waits for them, and re-layouts  1.03 us (1%)
  between operations  0.9 us (1%)
    ppermute x10, waiting for transfers between devices, swap(): return lax.ppermute(value, AXES, pairs)  24.7 us
    ppermute x10, starting transfers between devices, swap(): return lax.ppermute(value, AXES, pairs)  15.5 us
    pallas_call x4, Pallas kernels, factor_calls(): pl.pallas_call(functools.partial(factor_kernel, start), in_specs=[SMEM, V...  11.2 us
    ppermute x5, starting transfers between devices, halo_pair(): got.append(lax.ppermute(layer, axis, pairs))  6.04 us
    pallas_call x1, Pallas kernels, sketch_call(): pl.pallas_call(functools.partial(sketch_kernel, scale, steps), in_specs=[...  4.7 us
    pallas_call x1, Pallas kernels, finish_call(): pl.pallas_call(functools.partial(finish_kernel, steps), in_specs=[SMEM] +...  3.41 us
    pallas_call x1, Pallas kernels, operator_calls(): pl.pallas_call(functools.partial(operator_kernel, scale, range(half, cell...  2.67 us
    pallas_call x1, Pallas kernels, operator_calls(): pl.pallas_call(functools.partial(operator_kernel, scale, range(half)), in...  2.65 us
  transfers between devices with their start and end apart: 15, of which 7 were waited for; matrix products, arithmetic and copies ran while one was open for 0% of the time, Pallas kernels for 23%

profile of v1, /device:TPU:0, one launch (start us, length us, event | category | flops | bytes accessed | tf_op | source)
XLA Modules:
  0.0 73.0 jit_solution(3127182449247457780)
XLA Ops:
  0.7 0.1 pad_add_fusion.flag_ref.refs_0_
  0.7 4.7 %sketch.1 = (bf16[8,16,16,256]{3,2,1,0:T(8,128)(2,1)S(1)}, bf16[16,16,256]{2,1,0:T(8,128)(2,1)S(1)}, bf16[16,16,256]{2,1,0:T(8,128)(2,1)}, bf16[8,16,256]{2,1,0:...) custom-call(s32[4]{0:T(128)S(1)} %pad_add_fusion.flag_ref.refs_0_, ...), custom_call_target="tpu_custom_call" | custom-call | tf_op jit(solution)/shard_map/sketch/pallas_call | solution.py:126
  5.4 0.6 collective-permute-start.4
  6.0 0.7 collective-permute-start.5
  6.7 2.7 %collective-permute-start.6 = (bf16[8,16,256]{2,1,0:T(8,128)(2,1)S(1)}, bf16[8,16,256]{2,1,0:T(8,128)(2,1)S(1)}, u32[]{:S(2)}, u32[]{:S(2)}) collective-permute-start(bf16[8,16,256]{2,1,0:T(8,128)(2,1)S(1)} %get-tuple-element.29), channel_id=1, source_target_pairs={{0,1},{1,0},{2,3},{3,2},{4,5},{5,4},{6,7},{7,6},{8,9},{9,8},{10,11... | collective-permute-start | bytes 196616 | tf_op jit(solution)/shard_map/ppermute | solution.py:480
  9.3 2.6 %collective-permute-start = (f32[192,128]{1,0:T(8,128)S(1)}, f32[192,128]{1,0:T(8,128)S(1)}, u32[]{:S(2)}, u32[]{:S(2)}) collective-permute-start(f32[192,128]{1,0:T(8,128)S(1)} %get-tuple-element.24), channel_id=1, source_target_pairs={{0,4},{1,5},{2,6},{3,7},{4,0},{5,1},{6,2},{7,3},{8,12},{9,13},{10,... | collective-permute-start | bytes 294920 | tf_op jit(solution)/shard_map/ppermute | solution.py:441
  11.9 1.5 %collective-permute-start.3 = (bf16[16,16,256]{2,1,0:T(8,128)(2,1)S(1)}, bf16[16,16,256]{2,1,0:T(8,128)(2,1)S(1)}, u32[]{:S(2)}, u32[]{:S(2)}) collective-permute-start(bf16[16,16,256]{2,1,0:T(8,128)(2,1)S(1)} %get-tuple-element.26), channel_id=1, source_target_pairs={{0,16},{16,0},{1,17},{17,1},{2,18},{18,2},{3,19},{19,3},{4,20},{20... | collective-permute-start | bytes 393224 | tf_op jit(solution)/shard_map/ppermute | solution.py:480
  13.4 0.1 copy.6
  13.6 0.8 %copy-done.1 = f32[8,16,16]{2,1,0:T(8,128)S(1)} copy-done((f32[8,16,16]{2,1,0:T(8,128)S(1)}, f32[8,16,16]{2,1,0:T(8,128)}, u32[]{:S(2)}) %copy-start.1) | copy-done | bytes 8216
  14.4 0.1 copy.7
  14.5 0.7 collective-permute-start.7
  15.2 3.9 %collective-permute-start.1 = (f32[192,128]{1,0:T(8,128)S(1)}, f32[192,128]{1,0:T(8,128)S(1)}, u32[]{:S(2)}, u32[]{:S(2)}) collective-permute-start(f32[192,128]{1,0:T(8,128)S(1)} %add.45), channel_id=1, source_target_pairs={{0,2},{1,3},{2,0},{3,1},{4,12},{5,13},{6,14},{7,15},{8,10},{9,11},... | collective-permute-start | bytes 294920 | tf_op jit(solution)/shard_map/ppermute | solution.py:441
  19.2 2.6 %operator0.1 = (bf16[1024,512]{1,0:T(8,128)(2,1)S(1)}, f32[256,256]{1,0:T(8,128)S(1)}) custom-call(s32[4]{0:T(128)S(1)} %pad_add_fusion.flag_ref.refs_0_, bf16[8,16,16,256]{3,2,1,0:T(8,128)(2,1)S(1)} %get-tuple-element.25.s_ref, bf16[16,16,256]{2,1,0:T(8,128)(2,1)S(1)} %collective-permute-done.3.x1_ref, bf16[16,16,256]{2,1,0:T(8,128)(2,1)S(1)} %broadcast_in_dim.6.x2_ref, ...), custom_call_target="tpu_custom_call" | custom-call | tf_op jit(solution)/shard_map/operator0/pallas_call | solution.py:231
  21.8 2.7 %operator1.1 = (bf16[1024,512]{1,0:T(8,128)(2,1)S(1)}, f32[256,128]{1,0:T(8,128)S(1)}, f32[256,128]{1,0:T(8,128)S(1)}) custom-call(s32[4]{0:T(128)S(1)} %pad_add_fusion.flag_ref.refs_0_, bf16[8,16,16,256]{3,2,1,0:T(8,128)(2,1)S(1)} %get-tuple-element.25.s_ref, bf16[16,16,256]{2,1,0:T(8,128)(2,1)S(1)} %collective-permute-done.3.x1_ref, ...), custom_call_target="tpu_custom_call" | custom-call | tf_op jit(solution)/shard_map/operator1/pallas_call | solution.py:239
  24.6 0.9 %collective-permute-start.2 = (f32[192,128]{1,0:T(8,128)S(1)}, f32[192,128]{1,0:T(8,128)S(1)}, u32[]{:S(2)}, u32[]{:S(2)}) collective-permute-start(f32[192,128]{1,0:T(8,128)S(1)} %add.46), channel_id=1, source_target_pairs={{0,8},{1,9},{2,10},{3,11},{4,6},{5,7},{6,4},{7,5},{8,0},{9,1},{10,... | collective-permute-start | bytes 294920 | tf_op jit(solution)/shard_map/ppermute | solution.py:441
  25.5 0.4 collective-permute-done.8
  25.9 3.4 %collective-permute-done.2 = f32[192,128]{1,0:T(8,128)S(1)} collective-permute-done((f32[192,128]{1,0:T(8,128)S(1)}, f32[192,128]{1,0:T(8,128)S(1)}, u32[]{:S(2)}, u32[]{:S(2)}) %collective-permute-start.2) | collective-permute-done | bytes 98336 | tf_op jit(solution)/shard_map/ppermute | solution.py:441
  29.3 0.6 collective-permute-start.9
  29.9 5.5 %collective-permute-done.9 = f32[448,128]{1,0:T(8,128)S(1)} collective-permute-done((f32[448,128]{1,0:T(8,128)S(1)}, f32[448,128]{1,0:T(8,128)S(1)}, u32[]{:S(2)}, u32[]{:S(2)}) %collective-permute-start.9) | collective-permute-done | bytes 229408 | tf_op jit(solution)/shard_map/ppermute | solution.py:441
  35.4 2.7 %collective-permute-start.10 = (f32[448,128]{1,0:T(8,128)S(1)}, f32[448,128]{1,0:T(8,128)S(1)}, u32[]{:S(2)}, u32[]{:S(2)}) collective-permute-start(f32[448,128]{1,0:T(8,128)S(1)} %fusion), channel_id=1, source_target_pairs={{0,1},{1,0},{2,3},{3,2},{4,20},{5,21},{6,22},{7,23},{8,9},{9,8},{1... | collective-permute-start | bytes 688136 | tf_op jit(solution)/shard_map/ppermute | solution.py:441
  38.1 4.0 %collective-permute-done.10 = f32[448,128]{1,0:T(8,128)S(1)} collective-permute-done((f32[448,128]{1,0:T(8,128)S(1)}, f32[448,128]{1,0:T(8,128)S(1)}, u32[]{:S(2)}, u32[]{:S(2)}) %collective-permute-start.10) | collective-permute-done | bytes 229408 | tf_op jit(solution)/shard_map/ppermute | solution.py:441
  42.2 3.5 %collective-permute-start.11 = (f32[256,128]{1,0:T(8,128)S(1)}, f32[256,128]{1,0:T(8,128)S(1)}, u32[]{:S(2)}, u32[]{:S(2)}) collective-permute-start(f32[256,128]{1,0:T(8,128)S(1)} %slice.8), channel_id=1, source_target_pairs={{0,2},{1,3},{2,0},{3,1},{4,12},{5,13},{6,14},{7,15},{8,10},{9,11},... | collective-permute-start | bytes 393224 | tf_op jit(solution)/shard_map/ppermute | solution.py:441
  45.7 6.1 %collective-permute-done.11 = f32[256,128]{1,0:T(8,128)S(1)} collective-permute-done((f32[256,128]{1,0:T(8,128)S(1)}, f32[256,128]{1,0:T(8,128)S(1)}, u32[]{:S(2)}, u32[]{:S(2)}) %collective-permute-start.11) | collective-permute-done | bytes 131104 | tf_op jit(solution)/shard_map/ppermute | solution.py:441
  51.8 0.7 collective-permute-start.12
  52.5 4.3 %collective-permute-done.12 = f32[256,128]{1,0:T(8,128)S(1)} collective-permute-done((f32[256,128]{1,0:T(8,128)S(1)}, f32[256,128]{1,0:T(8,128)S(1)}, u32[]{:S(2)}, u32[]{:S(2)}) %collective-permute-start.12) | collective-permute-done | bytes 131104 | tf_op jit(solution)/shard_map/ppermute | solution.py:441
  56.9 0.5 collective-permute-start.14
  57.5 0.9 %collective-permute-done.14.refs_2_ = f32[192,128]{1,0:T(8,128)S(1)} collective-permute-done((f32[192,128]{1,0:T(8,128)S(1)}, f32[192,128]{1,0:T(8,128)S(1)}, u32[]{:S(2)}, u32[]{:S(2)}) %collective-permute-start.14) | collective-permute-done | bytes 98336 | tf_op jit(solution)/shard_map/ppermute | solution.py:441
  58.4 3.3 %shard_map.59 = (f32[64,256]{1,0:T(8,128)S(1)}, f32[192,256]{1,0:T(8,128)S(1)}) custom-call(s32[4]{0:T(128)S(1)} %pad_add_fusion.flag_ref.refs_0_, f32[192,128]{1,0:T(8,128)S(1)} %slice.9.refs_1_, f32[192,128]{1,0:T(8,128)S(1)} %collective-permute-done.14.refs_2_), custom_call_target="tpu_custom_call" | custom-call | tf_op jit(solution)/shard_map/pallas_call | solution.py:363
  61.7 2.8 %shard_map.60 = (f32[64,256]{1,0:T(8,128)S(1)}, f32[128,256]{1,0:T(8,128)S(1)}) custom-call(f32[192,256]{1,0:T(8,128)S(1)} %get-tuple-element.37.refs_0_), custom_call_target="tpu_custom_call" | custom-call | tf_op jit(solution)/shard_map/pallas_call | solution.py:363
  64.5 2.7 %shard_map.61 = (f32[64,256]{1,0:T(8,128)S(1)}, f32[64,256]{1,0:T(8,128)S(1)}) custom-call(f32[128,256]{1,0:T(8,128)S(1)} %get-tuple-element.39.refs_0_), custom_call_target="tpu_custom_call" | custom-call | tf_op jit(solution)/shard_map/pallas_call | solution.py:363
  67.1 2.5 %shard_map.62.refs_3_ = f32[64,256]{1,0:T(8,128)S(1)} custom-call(f32[64,256]{1,0:T(8,128)S(1)} %get-tuple-element.41.refs_0_), custom_call_target="tpu_custom_call" | custom-call | tf_op jit(solution)/shard_map/pallas_call | solution.py:363
  69.6 3.4 %finish.1 = (bf16[2048,256]{1,0:T(8,128)(2,1)}, f32[256,256]{1,0:T(8,128)}) custom-call(s32[4]{0:T(128)S(1)} %pad_add_fusion.flag_ref.refs_0_, f32[256,128]{1,0:T(8,128)S(1)} %add.52.part_ref, f32[256,128]{1,0:T(8,128)S(1)} %collective-permute-done.13.other_ref, bf16[1024,512]{1,0:T(8,128)(2,1)S(1)} %get-tuple-element.34.image0_ref, ...), custom_call_target="tpu_custom_call" | custom-call | tf_op jit(solution)/shard_map/finish/pallas_call | solution.py:416
  (27 shorter events, 0.4 us)
Async XLA Ops:
  0.7 12.7 %copy-start = (f32[3,8,16,16]{3,2,1,0:T(8,128)S(1)}, f32[3,8,16,16]{3,2,1,0:T(8,128)}, u32[]{:S(2)}) copy-start(f32[3,8,16,16]{3,2,1,0:T(8,128)} %param.6) | copy-start | bytes 73732
  5.4 9.7 %collective-permute-start.4 = (bf16[8,16,256]{2,1,0:T(8,128)(2,1)S(1)}, bf16[8,16,256]{2,1,0:T(8,128)(2,1)S(1)}, u32[]{:S(2)}, u32[]{:S(2)}) collective-permute-start(bf16[8,16,256]{2,1,0:T(8,128)(2,1)S(1)} %get-tuple-element.27), channel_id=1, source_target_pairs={{0,4},{4,0},{8,12},{12,8},{1,5},{5,1},{9,13},{13,9},{2,6},{6,2},{1... | collective-permute-start | bytes 196616 | tf_op jit(solution)/shard_map/ppermute | solution.py:480
  6.0 13.1 %collective-permute-start.5 = (bf16[8,16,256]{2,1,0:T(8,128)(2,1)S(1)}, bf16[8,16,256]{2,1,0:T(8,128)(2,1)S(1)}, u32[]{:S(2)}, u32[]{:S(2)}) collective-permute-start(bf16[8,16,256]{2,1,0:T(8,128)(2,1)S(1)} %get-tuple-element.28), channel_id=1, source_target_pairs={{4,8},{8,4},{5,9},{9,5},{6,10},{10,6},{7,11},{11,7},{20,24},{24,20... | collective-permute-start | bytes 196616 | tf_op jit(solution)/shard_map/ppermute | solution.py:480
  6.7 12.4 %collective-permute-start.6 = (bf16[8,16,256]{2,1,0:T(8,128)(2,1)S(1)}, bf16[8,16,256]{2,1,0:T(8,128)(2,1)S(1)}, u32[]{:S(2)}, u32[]{:S(2)}) collective-permute-start(bf16[8,16,256]{2,1,0:T(8,128)(2,1)S(1)} %get-tuple-element.29), channel_id=1, source_target_pairs={{0,1},{1,0},{2,3},{3,2},{4,5},{5,4},{6,7},{7,6},{8,9},{9,8},{10,11... | collective-permute-start | bytes 196616 | tf_op jit(solution)/shard_map/ppermute | solution.py:480
  9.3 5.1 %collective-permute-start = (f32[192,128]{1,0:T(8,128)S(1)}, f32[192,128]{1,0:T(8,128)S(1)}, u32[]{:S(2)}, u32[]{:S(2)}) collective-permute-start(f32[192,128]{1,0:T(8,128)S(1)} %get-tuple-element.24), channel_id=1, source_target_pairs={{0,4},{1,5},{2,6},{3,7},{4,0},{5,1},{6,2},{7,3},{8,12},{9,13},{10,... | collective-permute-start | bytes 294920 | tf_op jit(solution)/shard_map/ppermute | solution.py:441
  11.9 7.2 %collective-permute-start.3 = (bf16[16,16,256]{2,1,0:T(8,128)(2,1)S(1)}, bf16[16,16,256]{2,1,0:T(8,128)(2,1)S(1)}, u32[]{:S(2)}, u32[]{:S(2)}) collective-permute-start(bf16[16,16,256]{2,1,0:T(8,128)(2,1)S(1)} %get-tuple-element.26), channel_id=1, source_target_pairs={{0,16},{16,0},{1,17},{17,1},{2,18},{18,2},{3,19},{19,3},{4,20},{20... | collective-permute-start | bytes 393224 | tf_op jit(solution)/shard_map/ppermute | solution.py:480
  13.5 0.8 %copy-start.1 = (f32[8,16,16]{2,1,0:T(8,128)S(1)}, f32[8,16,16]{2,1,0:T(8,128)}, u32[]{:S(2)}) copy-start(f32[8,16,16]{2,1,0:T(8,128)} %param.7) | copy-start | bytes 24580
  14.5 4.7 %collective-permute-start.7 = (bf16[8,16,256]{2,1,0:T(8,128)(2,1)S(1)}, bf16[8,16,256]{2,1,0:T(8,128)(2,1)S(1)}, u32[]{:S(2)}, u32[]{:S(2)}) collective-permute-start(bf16[8,16,256]{2,1,0:T(8,128)(2,1)S(1)} %get-tuple-element.30), channel_id=1, source_target_pairs={{1,2},{2,1},{5,6},{6,5},{9,10},{10,9},{13,14},{14,13},{17,18},{18,... | collective-permute-start | bytes 196616 | tf_op jit(solution)/shard_map/ppermute | solution.py:480
  15.2 9.4 %collective-permute-start.1 = (f32[192,128]{1,0:T(8,128)S(1)}, f32[192,128]{1,0:T(8,128)S(1)}, u32[]{:S(2)}, u32[]{:S(2)}) collective-permute-start(f32[192,128]{1,0:T(8,128)S(1)} %add.45), channel_id=1, source_target_pairs={{0,2},{1,3},{2,0},{3,1},{4,12},{5,13},{6,14},{7,15},{8,10},{9,11},... | collective-permute-start | bytes 294920 | tf_op jit(solution)/shard_map/ppermute | solution.py:441
  24.5 1.4 %collective-permute-start.8 = (f32[256,128]{1,0:T(8,128)S(1)}, f32[256,128]{1,0:T(8,128)S(1)}, u32[]{:S(2)}, u32[]{:S(2)}) collective-permute-start(f32[256,128]{1,0:T(8,128)S(1)} %get-tuple-element.33), channel_id=1, source_target_pairs={{0,4},{1,5},{2,6},{3,7},{4,0},{5,1},{6,2},{7,3},{8,12},{9,13},{10,... | collective-permute-start | bytes 393224 | tf_op jit(solution)/shard_map/ppermute | solution.py:441
  24.6 4.7 %collective-permute-start.2 = (f32[192,128]{1,0:T(8,128)S(1)}, f32[192,128]{1,0:T(8,128)S(1)}, u32[]{:S(2)}, u32[]{:S(2)}) collective-permute-start(f32[192,128]{1,0:T(8,128)S(1)} %add.46), channel_id=1, source_target_pairs={{0,8},{1,9},{2,10},{3,11},{4,6},{5,7},{6,4},{7,5},{8,0},{9,1},{10,... | collective-permute-start | bytes 294920 | tf_op jit(solution)/shard_map/ppermute | solution.py:441
  29.3 6.1 %collective-permute-start.9 = (f32[448,128]{1,0:T(8,128)S(1)}, f32[448,128]{1,0:T(8,128)S(1)}, u32[]{:S(2)}, u32[]{:S(2)}) collective-permute-start(f32[448,128]{1,0:T(8,128)S(1)} %pad_maximum_fusion), channel_id=1, source_target_pairs={{0,16},{1,17},{2,18},{3,19},{4,5},{5,4},{6,7},{7,6},{8,24},{9,25},... | collective-permute-start | bytes 688136 | tf_op jit(solution)/shard_map/ppermute | solution.py:441
  35.4 6.7 %collective-permute-start.10 = (f32[448,128]{1,0:T(8,128)S(1)}, f32[448,128]{1,0:T(8,128)S(1)}, u32[]{:S(2)}, u32[]{:S(2)}) collective-permute-start(f32[448,128]{1,0:T(8,128)S(1)} %fusion), channel_id=1, source_target_pairs={{0,1},{1,0},{2,3},{3,2},{4,20},{5,21},{6,22},{7,23},{8,9},{9,8},{1... | collective-permute-start | bytes 688136 | tf_op jit(solution)/shard_map/ppermute | solution.py:441
  42.2 9.6 %collective-permute-start.11 = (f32[256,128]{1,0:T(8,128)S(1)}, f32[256,128]{1,0:T(8,128)S(1)}, u32[]{:S(2)}, u32[]{:S(2)}) collective-permute-start(f32[256,128]{1,0:T(8,128)S(1)} %slice.8), channel_id=1, source_target_pairs={{0,2},{1,3},{2,0},{3,1},{4,12},{5,13},{6,14},{7,15},{8,10},{9,11},... | collective-permute-start | bytes 393224 | tf_op jit(solution)/shard_map/ppermute | solution.py:441
  51.8 5.0 %collective-permute-start.12 = (f32[256,128]{1,0:T(8,128)S(1)}, f32[256,128]{1,0:T(8,128)S(1)}, u32[]{:S(2)}, u32[]{:S(2)}) collective-permute-start(f32[256,128]{1,0:T(8,128)S(1)} %slice_add_fusion), channel_id=1, source_target_pairs={{0,8},{1,9},{2,10},{3,11},{4,6},{5,7},{6,4},{7,5},{8,0},{9,1},{10,... | collective-permute-start | bytes 393224 | tf_op jit(solution)/shard_map/ppermute | solution.py:441
  56.8 12.8 %collective-permute-start.13 = (f32[256,128]{1,0:T(8,128)S(1)}, f32[256,128]{1,0:T(8,128)S(1)}, u32[]{:S(2)}, u32[]{:S(2)}) collective-permute-start(f32[256,128]{1,0:T(8,128)S(1)} %add.52.part_ref), channel_id=1, source_target_pairs={{0,4},{1,5},{2,6},{3,7},{4,0},{5,1},{6,2},{7,3},{8,12},{9,13},{10,... | collective-permute-start | bytes 393224 | tf_op jit(solution)/shard_map/ppermute | solution.py:441
  56.9 1.5 %collective-permute-start.14 = (f32[192,128]{1,0:T(8,128)S(1)}, f32[192,128]{1,0:T(8,128)S(1)}, u32[]{:S(2)}, u32[]{:S(2)}) collective-permute-start(f32[192,128]{1,0:T(8,128)S(1)} %slice.9.refs_1_), channel_id=1, source_target_pairs={{0,4},{1,5},{2,6},{3,7},{4,0},{5,1},{6,2},{7,3},{8,12},{9,13},{10,... | collective-permute-start | bytes 294920 | tf_op jit(solution)/shard_map/ppermute | solution.py:441
